TPU v7x, 512 devices: a whole 4x4x16 slice. The times are simulated.
512 devices in a mesh: row: 32 (over z, core), col: 16 (over x, y).
Axes of the slice: x: 4, y: 4, z: 16, core: 2. Of those that a mesh axis runs over, the one named last changes fastest.
Arguments:
- weight: bfloat16 [8192, 53248], P('row', 'col'), may hold values from -6 to 6
- inverse_rows: float32 [512, 53248], P('row', 'col'), as said below
- pruned_index: int32 [512], replicated, may hold values from 0 to 53247, as said below
Outputs:
- pruned_weight: bfloat16 [8192, 53248], P('row', 'col')
- saliency: float32 [8192], P('row')
Inputs may be any that keep to these rules, and one draw needn't show every extreme that they name: `pruned_index`: distinct and ascending. Neuron c lies in column shard c // 3328; at most 96 of them lie in one shard, and exactly 96 in one shard. `inverse_rows`: its columns pruned_index form a symmetric positive definite matrix.
All inputs are finite; a program needn't handle non-finite values.
Results may differ from a plain program's by a relative error of at most 0.001.
Values may be sent and summed in bfloat16 or wider, within the bound.
A program may use at most 64 MiB of HBM per device.

v0:
```python
import jax
import jax.numpy as jnp
from jax import lax
from jax.sharding import Mesh
from jax.sharding import PartitionSpec as P

ROW = ("row_0", "row_1")


def from_everyone(value, axis):
    count = lax.axis_size(axis)
    return lax.all_to_all(
        jnp.broadcast_to(value[None], (count, *value.shape)), axis, 0, 0, tiled=True
    )


def joined_along(parts, dim):
    parts = jnp.moveaxis(parts, 0, dim)
    shape = parts.shape
    return parts.reshape(*shape[:dim], shape[dim] * shape[dim + 1], *shape[dim + 2 :])


def gather_directly(value, axis, dim):
    parts = from_everyone(value, axis)
    return joined_along(parts, dim)


def all_blocks(value, axes, sequence):
    parts = value[None]
    for k in sequence:
        parts = lax.all_gather(parts, axes[k], axis=0, tiled=True)
    carried = [lax.axis_size(axes[k]) for k in reversed(sequence)]
    parts = parts.reshape(*carried, *value.shape)
    turned = sorted(range(len(sequence)), key=lambda place: sequence[len(sequence) - 1 - place])
    return parts.transpose(*turned, *range(len(sequence), parts.ndim)).reshape(-1, *value.shape)


def whole_of(value, axes, sequence, dim):
    return joined_along(all_blocks(value, axes, sequence), dim)


def body(weight, inverse_rows, pruned_index):
    row_count, col_width = weight.shape
    pruned_count = pruned_index.shape[0]
    col_devices = lax.axis_size("col")
    own_index = lax.axis_index("col")
    col_anchor = own_index * col_width
    capacity = 3 * pruned_count // col_devices
    boundary = jnp.arange(col_devices + 1, dtype=jnp.int32) * col_width
    edges_at = jnp.sum((pruned_index[None, :] < boundary[:, None]).astype(jnp.int32), axis=1)
    starts = edges_at[:-1]
    counts = edges_at[1:] - edges_at[:-1]
    window_start = starts[own_index]
    padded = jnp.concatenate([pruned_index, jnp.full((capacity,), -1, jnp.int32)])
    window = lax.dynamic_slice_in_dim(padded, window_start, capacity) - col_anchor
    slot_ids = jnp.arange(capacity, dtype=jnp.int32)
    occupied = slot_ids < counts[own_index]
    clipped = jnp.clip(window, 0, col_width - 1)
    column_ids = lax.broadcasted_iota(jnp.int32, (col_width, capacity), 0)
    picker = ((column_ids == clipped[None, :]) & occupied[None, :]).astype(jnp.bfloat16)
    weight_window = jnp.dot(weight, picker, preferred_element_type=jnp.float32).astype(jnp.bfloat16)
    inverse_window = jnp.where(occupied[None, :], jnp.take(inverse_rows, clipped, axis=1), 0.0)
    weight_all = gather_directly(weight_window, "col", 1)
    inverse_all = gather_directly(inverse_window, "col", 1)
    targets = (starts[:, None] + slot_ids[None, :]).reshape(-1)
    is_valid = (slot_ids[None, :] < counts[:, None]).reshape(-1)
    neuron_ids = lax.broadcasted_iota(jnp.int32, (col_devices * capacity, pruned_count), 1)
    placer = (neuron_ids == targets[:, None]) & is_valid[:, None]
    weight_pruned = jnp.dot(
        weight_all, placer.astype(jnp.bfloat16), preferred_element_type=jnp.float32
    )
    schur_part = jnp.dot(
        inverse_all,
        placer.astype(jnp.float32),
        precision=lax.Precision.HIGHEST,
        preferred_element_type=jnp.float32,
    )
    schur_block = whole_of(schur_part, ROW, (0, 1), 0)
    factor_low = jnp.linalg.cholesky(schur_block)
    solved = jax.scipy.linalg.cho_solve((factor_low, True), weight_pruned.T).T
    correction = jnp.dot(
        solved,
        lax.all_gather(inverse_rows, ROW, axis=0, tiled=True),
        precision=lax.Precision.HIGHEST,
        preferred_element_type=jnp.float32,
    )
    pruned_weight = (weight.astype(jnp.float32) - correction).astype(jnp.bfloat16)
    saliency = jnp.sum(solved * weight_pruned, axis=1) / (2.0 * pruned_count)
    return (pruned_weight, saliency)


def solution(mesh):
    split = Mesh(mesh.devices.reshape(16, 2, mesh.shape["col"]), ("row_0", "row_1", "col"))
    return jax.shard_map(
        body,
        mesh=split,
        in_specs=(P(ROW, "col"), P(ROW, "col"), P()),
        out_specs=(P(ROW, "col"), P(ROW)),
        check_vma=False,
    )
```

profile of v0, /device:TPU:8, one launch (start us, length us, event | category | flops | bytes accessed | tf_op | source)
XLA Modules:
  0.0 250.6 jit_solution(7870224598733661959)
XLA Ops:
  7.2 1.0 convert_reduce_fusion
  8.3 0.6 dynamic_slice.10
  10.1 0.7 dynamic_slice.9
  11.5 1.5 compare_and_fusion
  12.9 1.4 copy.33
  14.4 0.6 gather_fusion
  15.2 0.7 broadcast_in_dim.56
  15.8 9.1 %all-to-all-start = ((f32[16,16,96]{2,1,0:T(8,128)}), f32[16,16,96]{2,1,0:T(8,128)S(1)}, u32[]{:S(2)}, u32[]{:S(2)}) async-start(f32[16,16,96]{2,1,0:T(8,128)} %broadcast_in_dim.56), calls=%async_computation | async-start | bytes 262144 | tf_op jit(solution)/shard_map/all_to_all | solution.py:12
  25.3 6.1 %all-to-all-done = f32[16,16,96]{2,1,0:T(8,128)S(1)} async-done(((f32[16,16,96]{2,1,0:T(8,128)}), f32[16,16,96]{2,1,0:T(8,128)S(1)}, u32[]{:S(2)}, u32[]{:S(2)}) %all-to-all-start) | async-done | bytes 98336 | tf_op jit(solution)/shard_map/all_to_all | solution.py:12
  31.6 1.2 fusion.4
  32.8 39.3 %all-gather = f32[256,512]{1,0:T(8,128)} all-gather(f32[16,512]{1,0:T(8,128)S(1)} %fusion.4), channel_id=2, replica_groups=mesh['row_0'=16,'row_1'=2,'col'=16] {'row_0'}, dimensions={0}, use_global_device_ids=true | all-gather | bytes 557056 | tf_op jit(solution)/shard_map/all_gather | solution.py:31
  72.1 0.7 all-gather.6.cloned.1.call-update
  72.8 0.7 fusion.12
  73.5 1.0 broadcast_in_dim.58
  74.5 5.2 %all-to-all-start.1 = ((bf16[16,256,96]{1,2,0:T(8,128)(2,1)}), bf16[16,256,96]{1,2,0:T(8,128)(2,1)S(1)}, u32[]{:S(2)}, u32[]{:S(2)}) async-start(bf16[16,256,96]{1,2,0:T(8,128)(2,1)} %broadcast_in_dim.58), calls=%async_computation.1 | async-start | bytes 1572864 | tf_op jit(solution)/shard_map/all_to_all | solution.py:12
  79.7 10.0 %all-to-all-done.1 = bf16[16,256,96]{1,2,0:T(8,128)(2,1)S(1)} async-done(((bf16[16,256,96]{1,2,0:T(8,128)(2,1)}), bf16[16,256,96]{1,2,0:T(8,128)(2,1)S(1)}, u32[]{:S(2)}, u32[]{:S(2)}) %all-to-all-start.1) | async-done | bytes 786464 | tf_op jit(solution)/shard_map/all_to_all | solution.py:12
  89.7 2.0 fusion.2
  91.7 1.3 copy.36
  93.0 0.3 copy.37
  93.3 0.2 fusion.13
  93.6 11.7 %cholesky.104 = f32[128,128]{1,0:T(8,128)S(1)} custom-call(f32[128,128]{1,0:T(8,128)S(1)} %cholesky.266), custom_call_target="Cholesky" | custom-call | tf_op jit(solution)/shard_map/jit(cholesky)/cholesky | solution.py:79
  105.4 9.8 %custom-call.34 = f32[1,128,128]{1,2,0:T(8,128)S(1)} custom-call(f32[1,128,128]{2,1,0:T(8,128)S(1)} %get-tuple-element.31), custom_call_target="InvertDiagBlocksLowerTriangular" | custom-call | tf_op jit(solution)/shard_map/jit(cholesky)/cholesky | solution.py:79
  115.3 0.3 constant_dynamic-update-slice_fusion.3
  115.6 0.3 convolution_subtract_fusion.1
  115.9 11.7 %cholesky.217 = f32[128,128]{1,0:T(8,128)S(1)} custom-call(f32[128,128]{1,0:T(8,128)S(1)} %cholesky.270), custom_call_target="Cholesky" | custom-call | tf_op jit(solution)/shard_map/jit(cholesky)/cholesky | solution.py:79
  127.7 10.0 %custom-call.35 = f32[1,128,128]{1,2,0:T(8,128)S(1)} custom-call(f32[1,128,128]{2,1,0:T(8,128)S(1)} %get-tuple-element.28), custom_call_target="InvertDiagBlocksLowerTriangular" | custom-call | tf_op jit(solution)/shard_map/jit(cholesky)/cholesky | solution.py:79
  137.7 0.3 convolution_dynamic-update-slice_fusion
  138.0 0.4 convolution_subtract_fusion.6
  138.4 11.7 %cholesky.238 = f32[128,128]{1,0:T(8,128)S(1)} custom-call(f32[128,128]{1,0:T(8,128)S(1)} %cholesky.275), custom_call_target="Cholesky" | custom-call | tf_op jit(solution)/shard_map/jit(cholesky)/cholesky | solution.py:79
  150.1 9.8 %custom-call.36 = f32[1,128,128]{1,2,0:T(8,128)S(1)} custom-call(f32[1,128,128]{2,1,0:T(8,128)S(1)} %get-tuple-element.25), custom_call_target="InvertDiagBlocksLowerTriangular" | custom-call | tf_op jit(solution)/shard_map/jit(cholesky)/cholesky | solution.py:79
  159.9 0.2 convolution_dynamic-update-slice_fusion.1
  160.1 0.4 convolution_subtract_fusion.9
  160.5 11.9 %cholesky.255 = f32[128,128]{1,0:T(8,128)S(1)} custom-call(f32[128,128]{1,0:T(8,128)S(1)} %convolution_subtract_fusion.9), custom_call_target="Cholesky" | custom-call | tf_op jit(solution)/shard_map/jit(cholesky)/cholesky | solution.py:79
  172.5 0.6 compare_reduce_fusion.2
  173.1 0.7 compare_reduce_fusion.3
  175.1 0.7 compare_reduce_fusion.1
  176.5 0.7 compare_reduce_fusion
  178.1 8.2 %while.1 = (s32[]{:T(128)}, f32[512,512]{1,0:T(8,128)S(1)}, s32[4,2]{0,1:T(2,128)S(1)}, f32[4,128,128]{2,1,0:T(8,128)S(1)}, s32[]{:T(128)}) while((s32[]{:T(128)}, f32[512,512]{1,0:T(8,128)S(1)}, s32[4,2]{0,1:T(2,128)S(1)}, f32[4,128,128]{2,1,0:T(8,128)S(1)}, s32[]{:T(128)}) %tuple.33), condition=%wide.while_cond, body=%wide.while_body.sunk | while | flops 2 | bytes 131181 | solution.py:80
  178.2 0.6 fusion.84
  178.8 1.3 bitcast_dynamic-update-slice_fusion.2
  180.2 0.6 fusion.84
  180.8 1.3 bitcast_dynamic-update-slice_fusion.2
  182.2 0.6 fusion.84
  182.8 1.3 bitcast_dynamic-update-slice_fusion.2
  184.3 0.6 fusion.84
  184.9 1.3 bitcast_dynamic-update-slice_fusion.2
  186.2 39.3 %custom-call.37 = f32[4,128,128]{1,2,0:T(8,128)S(1)} custom-call(f32[4,128,128]{2,1,0:T(8,128)S(1)} %get-tuple-element.9), custom_call_target="InvertDiagBlocksLowerTriangular" | custom-call | tf_op jit(solution)/shard_map/jit(_cho_solve)/triangular_solve | solution.py:80
  225.6 0.3 fusion.42
  225.9 0.4 convolution_subtract_fusion.8
  226.3 0.3 fusion.55
  226.6 0.6 convolution_subtract_fusion.5
  227.2 0.3 fusion.57
  227.5 0.8 convolution_subtract_fusion.4
  228.3 0.3 fusion.59
  228.7 0.3 fusion.58
  229.0 0.3 convolution_subtract_fusion.7
  229.3 0.3 fusion.56
  229.7 0.4 convolution_subtract_fusion.3
  230.1 0.3 fusion.54
  230.5 0.5 convolution_subtract_fusion.2
  231.0 0.4 fusion.53
  231.4 0.1 fusion.17
  231.5 0.6 broadcast_multiply_fusion
  232.1 11.3 %fusion = bf16[256,3328]{1,0:T(8,128)(2,1)} fusion(f32[512,3328]{1,0:T(8,128)} %all-gather.6.cloned.1.call-done, bf16[256,3328]{1,0:T(8,128)(2,1)} %param.3, f32[128,256]{0,1:T(8,128)S(1)} %copy.44, f32[128,256]{0,1:T(8,128)S(1)} %copy.43, f32[128,256]{0,1:T(8,128)S(1)} %copy.42, f32[128,256]{0,1:T(8,128)S(1)} %fusion.53), kind=kOutput, calls=%fused_computation.4 | convolution fusion | flops 5237440512 | bytes 10747904 | tf_op jit(solution)/shard_map/dot_general | solution.py:81
  (40 shorter events, 1.8 us)
Async XLA Ops:
  7.2 65.7 %copy-start.1 = (bf16[256,3328]{1,0:T(8,128)(2,1)S(1)}, bf16[256,3328]{1,0:T(8,128)(2,1)}, u32[]{:S(2)}) copy-start(bf16[256,3328]{1,0:T(8,128)(2,1)} %param.3) | copy-start | bytes 5111812
  15.8 15.6 %all-to-all-start = ((f32[16,16,96]{2,1,0:T(8,128)}), f32[16,16,96]{2,1,0:T(8,128)S(1)}, u32[]{:S(2)}, u32[]{:S(2)}) async-start(f32[16,16,96]{2,1,0:T(8,128)} %broadcast_in_dim.56), calls=%async_computation | async-start | bytes 262144 | tf_op jit(solution)/shard_map/all_to_all | solution.py:12
  24.9 66.7 %all-gather.4.cloned.1.call-start = ((), (), s32[]{:S(2)}) async-start(), calls=%async_computation.2 | async-start | bytes 1572864 | tf_op jit(solution)/shard_map/all_gather | solution.py:31
  72.1 160.0 %all-gather.6.cloned.1.call-start = ((), (), s32[]{:S(2)}) async-start(), calls=%async_computation.3 | async-start | bytes 7028736 | tf_op jit(solution)/shard_map/all_gather | solution.py:83
  74.5 15.2 %all-to-all-start.1 = ((bf16[16,256,96]{1,2,0:T(8,128)(2,1)}), bf16[16,256,96]{1,2,0:T(8,128)(2,1)S(1)}, u32[]{:S(2)}, u32[]{:S(2)}) async-start(bf16[16,256,96]{1,2,0:T(8,128)(2,1)} %broadcast_in_dim.58), calls=%async_computation.1 | async-start | bytes 1572864 | tf_op jit(solution)/shard_map/all_to_all | solution.py:12
  115.2 110.3 %copy-start = (f32[256,512]{1,0:T(8,128)S(1)}, f32[256,512]{1,0:T(8,128)}, u32[]{:S(2)}) copy-start(f32[256,512]{1,0:T(8,128)} %fusion.2) | copy-start | bytes 1572868
Sparse Core Ops, SparseCore 0:
  72.2 12.8 all-gather.3
  87.2 78.7 all-gather.5
where the time goes:
time: 254 us; the launch traced here: 251 us
  other arithmetic  123 us (48%)
  blocking collectives  39.3 us (15%)
  matrix products  22.5 us (9%)
  between operations  19.5 us (8%)
  waiting for transfers between devices  16.8 us (7%)
  local copies, waits for them, and re-layouts  15.4 us (6%)
  starting transfers between devices  14.4 us (6%)
    another operation x15, other arithmetic, body(): factor_low = jnp.linalg.cholesky(schur_block)  79.6 us
    another operation x3, other arithmetic, body(): solved = jax.scipy.linalg.cho_solve((factor_low, True), weight_pruned.T).T  39.4 us
    all_gather x1, blocking collectives, all_blocks(): parts = lax.all_gather(parts, axes[k], axis=0, tiled=True)  39.3 us
    all_to_all x2, waiting for transfers between devices, from_everyone(): lax.all_to_all(jnp.broadcast_to(value[None], (count, *value.shape)), axis...  16.1 us
    all_to_all x2, starting transfers between devices, from_everyone(): lax.all_to_all(jnp.broadcast_to(value[None], (count, *value.shape)), axis...  14.3 us
    dot_general x1, matrix products, body(): jnp.dot(solved, lax.all_gather(inverse_rows, ROW, axis=0, tiled=True), pr...  11.3 us
    another operation x12, local copies, waits for them, and re-layouts  8.07 us
    another operation x14, matrix products, body(): solved = jax.scipy.linalg.cho_solve((factor_low, True), weight_pruned.T).T  5.41 us
  transfers between devices with their start and end apart: 4, of which 2 were waited for; matrix products, arithmetic and copies ran while one was open for 56% of the time, Pallas kernels for 0%

commit v1 on v0

v1 whole, which is shorter than its diff:
```python
import functools

import jax
import jax.numpy as jnp
from jax import lax
from jax.experimental import pallas as pl
from jax.experimental.pallas import tpu as pltpu
from jax.sharding import PartitionSpec as P

F32, BF16 = jnp.float32, jnp.bfloat16
LANES = 128


def split3(x):
    hi = x.astype(BF16)
    r = x - hi.astype(F32)
    mid = r.astype(BF16)
    lo = (r - mid.astype(F32)).astype(BF16)
    return hi, mid, lo

def bsub(x, k):
    return jnp.broadcast_to(x[k:k+1, :], x.shape)

def inv8(cols):
    sub = lax.broadcasted_iota(jnp.int32, (8, 128), 0)
    for k in range(8):
        t = [bsub(c, k) for c in cols]
        r = 1.0 / t[k]
        ck = cols[k]
        new = []
        for j in range(8):
            if j == k:
                new.append(jnp.where(sub == k, r, -(ck * r)))
            else:
                new.append(jnp.where(sub == k, t[j] * r, cols[j] - (ck * t[j]) * r))
        cols = new
    return cols

def panel_gj(P, kb, nb, nt):
    lane = lax.broadcasted_iota(jnp.int32, (8, 128), 1)
    sub = lax.broadcasted_iota(jnp.int32, (8, 128), 0)
    for g in range(nb):
        col0 = kb + g * 8
        pt, l0 = col0 // 128, col0 % 128
        C = [[jnp.broadcast_to(P[i][pt][:, l0 + j:l0 + j + 1], (8, 128)) for j in range(8)] for i in range(nb)]
        Dinv = inv8(C[g])
        inside = (lane >= l0) & (lane < l0 + 8)
        eye = jnp.where(lane - l0 == sub, 1.0, 0.0)
        for i in range(nb):
            P[i][pt] = jnp.where(inside, eye if i == g else 0.0, P[i][pt])
        U = []
        for t in range(nt):
            acc = Dinv[0] * bsub(P[g][t], 0)
            for j in range(1, 8):
                acc = acc + Dinv[j] * bsub(P[g][t], j)
            U.append(acc)
        for t in range(nt):
            ub = [bsub(U[t], j) for j in range(8)]
            for i in range(nb):
                if i != g:
                    acc = P[i][t]
                    for j in range(8):
                        acc = acc - C[i][j] * ub[j]
                    P[i][t] = acc
            P[g][t] = U[t]
    return P

def solve_kernel(s_ref, w_ref, hi_ref, lo_ref, sal_ref, m, *, B=32, n=512):
    nw = w_ref.shape[0]
    nb, nt = B // 8, n // 128
    m[0:n, :] = s_ref[...]
    m[n:n + nw, :] = w_ref[...].astype(F32)
    rows = n + nw
    lane = lax.broadcasted_iota(jnp.int32, (8, 128), 1)
    sub = lax.broadcasted_iota(jnp.int32, (8, 128), 0)
    def load_panel(k):
        return [[m[k*B+g*8:k*B+g*8+8, t*128:t*128+128] for t in range(nt)] for g in range(nb)]
    P = load_panel(0)
    for k in range(n // B):
        kb = k * B
        P = panel_gj(P, kb, nb, nt)
        pt, l0 = kb // 128, kb % 128
        for g in range(nb):
            x = P[g][pt]
            inside = (lane >= l0) & (lane < l0 + B)
            eye = jnp.where(lane - l0 == sub + g * 8, 1.0, 0.0)
            P[g][pt] = jnp.where(inside, eye - x, x)
        U = jnp.concatenate([jnp.concatenate(P[g], axis=1) for g in range(nb)], axis=0)
        uh, um, ul = split3(U)
        us = jnp.concatenate([uh, um, uh, ul, um, uh], axis=0)
        def upd(r0, r1):
            C = m[r0:r1, pt*128:pt*128+128][:, l0:l0 + B]
            ch, cm, cl = split3(C)
            cs = jnp.concatenate([ch, ch, cm, ch, cm, cl], axis=1)
            return m[r0:r1, :] - jnp.dot(cs, us, preferred_element_type=F32)
        nr0 = (k + 1) * B
        if k + 1 < n // B:
            new = upd(nr0, nr0 + B)
            P = [[new[g*8:g*8+8, t*128:t*128+128] for t in range(nt)] for g in range(nb)]
            nr0 += B
        m[nr0:rows, :] = upd(nr0, rows)
    X = m[n:rows, :]
    h = X.astype(BF16)
    hi_ref[...] = h
    lo_ref[...] = (X - h.astype(F32)).astype(BF16)
    sal_ref[...] = jnp.sum(X * w_ref[...].astype(F32), axis=1, keepdims=True) / (2.0 * n)

def solve(S, W, B=32):
    n, nw = S.shape[0], W.shape[0]
    return pl.pallas_call(
        functools.partial(solve_kernel, B=B, n=n),
        out_shape=(jax.ShapeDtypeStruct((nw, n), BF16), jax.ShapeDtypeStruct((nw, n), BF16), jax.ShapeDtypeStruct((nw, 1), F32)),
        in_specs=[pl.BlockSpec(memory_space=pltpu.VMEM)] * 2,
        out_specs=tuple(pl.BlockSpec(memory_space=pltpu.VMEM) for _ in range(3)),
        scratch_shapes=[pltpu.VMEM((n + nw, n), F32)],
        name="solve",
    )(S, W)

MESH_ID = pl.DeviceIdType.MESH


def exchange_kernel(idx_ref, w_ref, inv_ref, s_out, wsel_out, sbuf, wbuf, place, sblk,
                    xs_send, xs_recv, xw_send, xw_recv, up_send, up_recv, dn_send, dn_recv, pr_send, pr_recv):
    n_row, n_col = lax.axis_size("row"), lax.axis_size("col")
    n_z = n_row // 2
    rows, width = w_ref.shape
    n = idx_ref.shape[1]
    row, col = lax.axis_index("row"), lax.axis_index("col")
    z, core = row // 2, lax.rem(row, 2)
    up = lax.rem(row + 2, n_row)
    down = lax.rem(row + n_row - 2, n_row)
    partner = row + 1 - 2 * core

    barrier = pltpu.get_barrier_semaphore()
    for k in range(1, n_col):
        pl.semaphore_signal(barrier, inc=1, device_id={"row": row, "col": lax.rem(col + k, n_col)}, device_id_type=MESH_ID)
    for other in (up, down, partner):
        pl.semaphore_signal(barrier, inc=1, device_id={"row": other, "col": col}, device_id_type=MESH_ID)

    idx = idx_ref[...]
    anchor = col * width
    start = jnp.sum(jnp.where(idx < anchor, 1.0, 0.0), axis=1, keepdims=True)
    own = jnp.where((idx >= anchor) & (idx < anchor + width), 1.0, 0.0)
    high = idx // 256
    low = idx - high * 256
    sub8 = lax.broadcasted_iota(jnp.int32, (8, n), 0)
    facts = jnp.where(sub8 == 0, high.astype(F32), jnp.where(sub8 == 1, low.astype(F32), jnp.where(sub8 == 2, own, 0.0)))
    at = lax.broadcasted_iota(jnp.int32, (n, LANES), 0).astype(F32)
    slot = lax.broadcasted_iota(jnp.int32, (n, LANES), 1).astype(F32)
    window = jnp.where(at == slot + start, 1.0, 0.0).astype(BF16)
    picked = jnp.dot(facts.astype(BF16), window, preferred_element_type=F32)
    local = jnp.where(picked[2:3, :] > 0.5, picked[0:1, :] * 256.0 + picked[1:2, :] - anchor.astype(F32), -1.0)
    column = lax.broadcasted_iota(jnp.int32, (width, LANES), 0).astype(F32)
    picker = jnp.where(column == local, 1.0, 0.0).astype(BF16)

    ih, im, il = split3(inv_ref[...])
    part = inv_ref.shape[0]
    three = jnp.dot(jnp.concatenate([ih, im, il], axis=0), picker, preferred_element_type=F32)
    sbuf[col] = three[0:part] + three[part:2 * part] + three[2 * part:3 * part]
    wbuf[col] = jnp.dot(w_ref[...], picker, preferred_element_type=F32).astype(BF16)

    pl.semaphore_wait(barrier, n_col + 2)
    s_copies, w_copies = [], []
    for k in range(1, n_col):
        target = {"row": row, "col": lax.rem(col + k, n_col)}
        c = pltpu.make_async_remote_copy(sbuf.at[col], sbuf.at[col], xs_send.at[k], xs_recv.at[k], device_id=target, device_id_type=MESH_ID)
        c.start()
        s_copies.append(c)
    for k in range(1, n_col):
        target = {"row": row, "col": lax.rem(col + k, n_col)}
        c = pltpu.make_async_remote_copy(wbuf.at[col], wbuf.at[col], xw_send.at[k], xw_recv.at[k], device_id=target, device_id_type=MESH_ID)
        c.start()
        w_copies.append(c)

    shard = lax.broadcasted_iota(jnp.int32, (n_col, n), 0)
    starts = jnp.sum(jnp.where(idx < shard * width, 1.0, 0.0), axis=1, keepdims=True)
    mine = (idx >= shard * width) & (idx < (shard + 1) * width)
    base = jnp.sum(jnp.where(mine, (shard * LANES).astype(F32) - starts, 0.0), axis=0, keepdims=True)
    slot_of = base + lax.broadcasted_iota(jnp.int32, (1, n), 1).astype(F32)
    for c in range(n_col):
        q = lax.broadcasted_iota(jnp.int32, (LANES, n), 0).astype(F32) + float(c * LANES)
        place[c * LANES:(c + 1) * LANES, :] = jnp.where(q == slot_of, 1.0, 0.0).astype(BF16)

    for c in s_copies:
        c.wait()
    joined = jnp.concatenate([sbuf[c] for c in range(n_col)], axis=1)
    jh, jm, jl = split3(joined)
    three = jnp.dot(jnp.concatenate([jh, jm, jl], axis=0), place[...], preferred_element_type=F32)
    sblk[z, core] = three[0:part] + three[part:2 * part] + three[2 * part:3 * part]

    def send(block, owner_core, target_row, send_sem, recv_sem):
        c = pltpu.make_async_remote_copy(sblk.at[block, owner_core], sblk.at[block, owner_core], send_sem, recv_sem,
                                         device_id={"row": target_row, "col": col}, device_id_type=MESH_ID)
        c.start()
        return c
    ups, downs = n_z // 2, n_z - 1 - n_z // 2
    held = [send(z, core, partner, pr_send.at[0], pr_recv.at[0])]
    flying_up = send(z, core, up, up_send.at[0], up_recv.at[0])
    flying_dn = send(z, core, down, dn_send.at[0], dn_recv.at[0])
    for s in range(1, ups + 1):
        block = lax.rem(z + n_z - s, n_z)
        flying_up.wait()
        if s < ups:
            flying_up = send(block, core, up, up_send.at[s], up_recv.at[s])
        held.append(send(block, core, partner, pr_send.at[s], pr_recv.at[s]))
        if s <= downs:
            block = lax.rem(z + s, n_z)
            flying_dn.wait()
            if s < downs:
                flying_dn = send(block, core, down, dn_send.at[s], dn_recv.at[s])
            held.append(send(block, core, partner, pr_send.at[ups + s], pr_recv.at[ups + s]))
    for c in w_copies:
        c.wait()
    wj = jnp.concatenate([wbuf[c] for c in range(n_col)], axis=1)
    wsel_out[...] = jnp.dot(wj, place[...], preferred_element_type=F32).astype(BF16)
    for c in held:
        c.wait()
    for b in range(n_z):
        for c in range(2):
            r0 = (b * 2 + c) * part
            s_out[r0:r0 + part, :] = sblk[b, c]


def exchange(idx, weight, inverse_rows, n_row, n_col):
    n = idx.shape[1]
    rows, part = weight.shape[0], inverse_rows.shape[0]
    n_z = n_row // 2
    dma = pltpu.SemaphoreType.DMA
    vm = pl.BlockSpec(memory_space=pltpu.VMEM)
    return pl.pallas_call(
        exchange_kernel,
        out_shape=(jax.ShapeDtypeStruct((n, n), F32), jax.ShapeDtypeStruct((rows, n), BF16)),
        in_specs=[vm] * 3,
        out_specs=(vm, vm),
        scratch_shapes=[
            pltpu.VMEM((n_col, part, LANES), F32),
            pltpu.VMEM((n_col, rows, LANES), BF16),
            pltpu.VMEM((n_col * LANES, n), BF16),
            pltpu.VMEM((n_z, 2, part, n), F32),
            dma((n_col,)), dma((n_col,)), dma((n_col,)), dma((n_col,)),
            dma((n_z,)), dma((n_z,)), dma((n_z,)), dma((n_z,)), dma((n_z,)), dma((n_z,)),
        ],
        compiler_params=pltpu.CompilerParams(collective_id=0, has_side_effects=True),
        name="exchange",
    )(idx, weight, inverse_rows)


def update_kernel(w_ref, inv_ref, hi_ref, lo_ref, out_ref):
    inv = inv_ref[...]
    ih = inv.astype(BF16)
    il = (inv - ih.astype(F32)).astype(BF16)
    hi, lo = hi_ref[...], lo_ref[...]
    left = jnp.concatenate([hi, lo, hi], axis=1)
    right = jnp.concatenate([ih, ih, il], axis=0)
    out_ref[...] = (w_ref[...].astype(F32) - jnp.dot(left, right, preferred_element_type=F32)).astype(BF16)


def update(weight, inverse_all, hi, lo, tile=256):
    rows, width = weight.shape
    n = hi.shape[1]
    return pl.pallas_call(
        update_kernel,
        grid=(width // tile,),
        out_shape=jax.ShapeDtypeStruct((rows, width), BF16),
        in_specs=[pl.BlockSpec((rows, tile), lambda i: (0, i)), pl.BlockSpec((n, tile), lambda i: (0, i)),
                  pl.BlockSpec((rows, n), lambda i: (0, 0)), pl.BlockSpec((rows, n), lambda i: (0, 0))],
        out_specs=pl.BlockSpec((rows, tile), lambda i: (0, i)),
        name="update",
    )(weight, inverse_all, hi, lo)


def solution(mesh):
    n_row, n_col = mesh.shape["row"], mesh.shape["col"]

    def body(weight, inverse_rows, pruned_index):
        inverse_all = lax.all_gather(inverse_rows, "row", axis=0, tiled=True)
        schur, chosen = exchange(pruned_index[None, :], weight, inverse_rows, n_row, n_col)
        hi, lo, sal = solve(schur, chosen)
        return update(weight, inverse_all, hi, lo), sal[:, 0]

    return jax.shard_map(
        body,
        mesh=mesh,
        in_specs=(P("row", "col"), P("row", "col"), P()),
        out_specs=(P("row", "col"), P("row")),
        check_vma=False,
    )
```

time: 254 us -> 113 us (0.44)
  the two profiles are of different devices: /device:TPU:8 before, /device:TPU:1 now
where the time goes in v1:
time: 113 us
  Pallas kernels  95.2 us (84%)
  between operations  14 us (12%)
  waiting for transfers between devices  1.93 us (2%)
  other arithmetic  1.58 us (1%)
    pallas_call x1, Pallas kernels, exchange(): pl.pallas_call(exchange_kernel, out_shape=(jax.ShapeDtypeStruct((n, n), F...  62.9 us
    pallas_call x1, Pallas kernels, solve(): pl.pallas_call(functools.partial(solve_kernel, B=B, n=n), out_shape=(jax....  20.7 us
    pallas_call x1, Pallas kernels, update(): pl.pallas_call(update_kernel, grid=(width // tile,), out_shape=jax.ShapeD...  11.7 us
  transfers between devices with their start and end apart: 1, of which 1 were waited for; matrix products, arithmetic and copies ran while one was open for 1% of the time, Pallas kernels for 74%

profile of v1, /device:TPU:1, one launch (start us, length us, event | category | flops | bytes accessed | tf_op | source)
XLA Modules:
  0.0 112.8 jit_solution(7087667480927442039)
XLA Ops:
  7.2 0.0 all-gather.2.cloned.1.call-start
  7.2 0.7 all-gather.2.cloned.1.call-update
  7.9 62.9 %exchange.1 = (f32[512,512]{1,0:T(8,128)}, bf16[256,512]{1,0:T(8,128)(2,1)}) custom-call(s32[1,512]{1,0:T(1,128)} %bitcast.1, bf16[256,3328]{1,0:T(8,128)(2,1)} %w_ref.3, f32[16,3328]{1,0:T(8,128)} %inv_ref.1), custom_call_target="tpu_custom_call" | custom-call | tf_op jit(solution)/shard_map/exchange/pallas_call | solution.py:230
  70.8 20.7 %solve.1 = (bf16[256,512]{1,0:T(8,128)(2,1)}, bf16[256,512]{1,0:T(8,128)(2,1)}, f32[256,1]{1,0:T(8,128)}) custom-call(f32[512,512]{1,0:T(8,128)} %get-tuple-element.7.s_ref, bf16[256,512]{1,0:T(8,128)(2,1)} %get-tuple-element.8.w_ref), custom_call_target="tpu_custom_call" | custom-call | tf_op jit(solution)/shard_map/solve/pallas_call | solution.py:110
  91.4 1.6 %reduce = f32[256]{0:T(256)} reduce(f32[256,1]{1,0:T(8,128)} %get-tuple-element.11, f32[]{:T(128)} %constant.1), dimensions={1}, to_apply=%get-tuple-element.11.reduce_sub_computation | reduce | bytes 2052 | tf_op jit(solution)/shard_map/solve/pallas_call | solution.py:110
  93.0 1.2 %all-gather.2.cloned.1.call-done.inv_ref = f32[512,3328]{1,0:T(8,128)} async-done(((f32[16,3328]{1,0:T(8,128)}), f32[512,3328]{1,0:T(8,128)}) %all-gather.2.cloned.1.call-update) | async-done | bytes 6815760 | tf_op jit(solution)/shard_map/all_gather | solution.py:276
  94.3 11.7 %update.1 = bf16[256,3328]{1,0:T(8,128)(2,1)} custom-call(bf16[256,3328]{1,0:T(8,128)(2,1)} %w_ref.3, f32[512,3328]{1,0:T(8,128)} %all-gather.2.cloned.1.call-done.inv_ref, bf16[256,512]{1,0:T(8,128)(2,1)} %get-tuple-element.9.hi_ref, bf16[256,512]{1,0:T(8,128)(2,1)} %get-tuple-element.10.lo_ref), custom_call_target="tpu_custom_call" | custom-call | tf_op jit(solution)/shard_map/update/pallas_call | solution.py:261
Async XLA Ops:
  7.2 87.1 %all-gather.2.cloned.1.call-start = ((), (), s32[]{:S(2)}) async-start(), calls=%async_computation | async-start | bytes 7028736 | tf_op jit(solution)/shard_map/all_gather | solution.py:276
Sparse Core Ops, SparseCore 0:
  10.1 84.1 all-gather.1

commit v2 on v1

--- a/solution.py
+++ b/solution.py
@@ -9,6 +9,7 @@
 
 F32, BF16 = jnp.float32, jnp.bfloat16
 LANES = 128
+BLOCK = 32
 
 
 def split3(x):
@@ -65,62 +66,45 @@
             P[g][t] = U[t]
     return P
 
-def solve_kernel(s_ref, w_ref, hi_ref, lo_ref, sal_ref, m, *, B=32, n=512):
-    nw = w_ref.shape[0]
-    nb, nt = B // 8, n // 128
-    m[0:n, :] = s_ref[...]
-    m[n:n + nw, :] = w_ref[...].astype(F32)
-    rows = n + nw
+
+def eliminate(m, n, after):
+    rows = m.shape[0]
+    nb, nt = BLOCK // 8, n // 128
     lane = lax.broadcasted_iota(jnp.int32, (8, 128), 1)
     sub = lax.broadcasted_iota(jnp.int32, (8, 128), 0)
-    def load_panel(k):
-        return [[m[k*B+g*8:k*B+g*8+8, t*128:t*128+128] for t in range(nt)] for g in range(nb)]
-    P = load_panel(0)
-    for k in range(n // B):
-        kb = k * B
+    P = [[m[g*8:g*8+8, t*128:t*128+128] for t in range(nt)] for g in range(nb)]
+    for k in range(n // BLOCK):
+        kb = k * BLOCK
         P = panel_gj(P, kb, nb, nt)
         pt, l0 = kb // 128, kb % 128
         for g in range(nb):
             x = P[g][pt]
-            inside = (lane >= l0) & (lane < l0 + B)
+            inside = (lane >= l0) & (lane < l0 + BLOCK)
             eye = jnp.where(lane - l0 == sub + g * 8, 1.0, 0.0)
             P[g][pt] = jnp.where(inside, eye - x, x)
         U = jnp.concatenate([jnp.concatenate(P[g], axis=1) for g in range(nb)], axis=0)
         uh, um, ul = split3(U)
         us = jnp.concatenate([uh, um, uh, ul, um, uh], axis=0)
+
         def upd(r0, r1):
-            C = m[r0:r1, pt*128:pt*128+128][:, l0:l0 + B]
+            C = m[r0:r1, pt*128:pt*128+128][:, l0:l0 + BLOCK]
             ch, cm, cl = split3(C)
             cs = jnp.concatenate([ch, ch, cm, ch, cm, cl], axis=1)
             return m[r0:r1, :] - jnp.dot(cs, us, preferred_element_type=F32)
-        nr0 = (k + 1) * B
-        if k + 1 < n // B:
-            new = upd(nr0, nr0 + B)
+        nr0 = (k + 1) * BLOCK
+        if k + 1 < n // BLOCK:
+            new = upd(nr0, nr0 + BLOCK)
             P = [[new[g*8:g*8+8, t*128:t*128+128] for t in range(nt)] for g in range(nb)]
-            nr0 += B
+            nr0 += BLOCK
         m[nr0:rows, :] = upd(nr0, rows)
-    X = m[n:rows, :]
-    h = X.astype(BF16)
-    hi_ref[...] = h
-    lo_ref[...] = (X - h.astype(F32)).astype(BF16)
-    sal_ref[...] = jnp.sum(X * w_ref[...].astype(F32), axis=1, keepdims=True) / (2.0 * n)
-
-def solve(S, W, B=32):
-    n, nw = S.shape[0], W.shape[0]
-    return pl.pallas_call(
-        functools.partial(solve_kernel, B=B, n=n),
-        out_shape=(jax.ShapeDtypeStruct((nw, n), BF16), jax.ShapeDtypeStruct((nw, n), BF16), jax.ShapeDtypeStruct((nw, 1), F32)),
-        in_specs=[pl.BlockSpec(memory_space=pltpu.VMEM)] * 2,
-        out_specs=tuple(pl.BlockSpec(memory_space=pltpu.VMEM) for _ in range(3)),
-        scratch_shapes=[pltpu.VMEM((n + nw, n), F32)],
-        name="solve",
-    )(S, W)
+        after(k)
 
 MESH_ID = pl.DeviceIdType.MESH
 
 
-def exchange_kernel(idx_ref, w_ref, inv_ref, s_out, wsel_out, sbuf, wbuf, place, sblk,
-                    xs_send, xs_recv, xw_send, xw_recv, up_send, up_recv, dn_send, dn_recv, pr_send, pr_recv):
+def step_kernel(idx_ref, w_ref, inv_ref, out_ref, sal_ref, sbuf, wbuf, place, sblk, m, gat, outv,
+                xs_send, xs_recv, xw_send, xw_recv, up_send, up_recv, dn_send, dn_recv, pr_send, pr_recv,
+                gu_send, gu_recv, gd_send, gd_recv, gp_send, gp_recv, out_sem):
     n_row, n_col = lax.axis_size("row"), lax.axis_size("col")
     n_z = n_row // 2
     rows, width = w_ref.shape
@@ -155,11 +139,21 @@
 
     ih, im, il = split3(inv_ref[...])
     part = inv_ref.shape[0]
+    gat[0, z, core] = ih
+    gat[1, z, core] = im
     three = jnp.dot(jnp.concatenate([ih, im, il], axis=0), picker, preferred_element_type=F32)
     sbuf[col] = three[0:part] + three[part:2 * part] + three[2 * part:3 * part]
     wbuf[col] = jnp.dot(w_ref[...], picker, preferred_element_type=F32).astype(BF16)
 
     pl.semaphore_wait(barrier, n_col + 2)
+    ups, downs = n_z // 2, n_z - 1 - n_z // 2
+    sent = []
+
+    def push(p, block, target_row, send_sem, recv_sem):
+        c = pltpu.make_async_remote_copy(gat.at[p, block, core], gat.at[p, block, core], send_sem, recv_sem,
+                                         device_id={"row": target_row, "col": col}, device_id_type=MESH_ID)
+        c.start()
+        return c
     s_copies, w_copies = [], []
     for k in range(1, n_col):
         target = {"row": row, "col": lax.rem(col + k, n_col)}
@@ -171,6 +165,26 @@
         c = pltpu.make_async_remote_copy(wbuf.at[col], wbuf.at[col], xw_send.at[k], xw_recv.at[k], device_id=target, device_id_type=MESH_ID)
         c.start()
         w_copies.append(c)
+
+    fly_up, fly_dn, mates = {}, {}, []
+    for p in range(2):
+        fly_up[p] = push(p, z, up, gu_send.at[p, 0], gu_recv.at[p, 0])
+        fly_dn[p] = push(p, z, down, gd_send.at[p, 0], gd_recv.at[p, 0])
+        mates.append(push(p, z, partner, gp_send.at[p, 0], gp_recv.at[p, 0]))
+
+    def service(piece):
+        s, p = piece // 2 + 1, piece % 2
+        block = lax.rem(z + n_z - s, n_z)
+        fly_up[p].wait()
+        if s < ups:
+            fly_up[p] = push(p, block, up, gu_send.at[p, s], gu_recv.at[p, s])
+        mates.append(push(p, block, partner, gp_send.at[p, s], gp_recv.at[p, s]))
+        if s <= downs:
+            block = lax.rem(z + s, n_z)
+            fly_dn[p].wait()
+            if s < downs:
+                fly_dn[p] = push(p, block, down, gd_send.at[p, s], gd_recv.at[p, s])
+            mates.append(push(p, block, partner, gp_send.at[p, ups + s], gp_recv.at[p, ups + s]))
 
     shard = lax.broadcasted_iota(jnp.int32, (n_col, n), 0)
     starts = jnp.sum(jnp.where(idx < shard * width, 1.0, 0.0), axis=1, keepdims=True)
@@ -193,7 +207,6 @@
                                          device_id={"row": target_row, "col": col}, device_id_type=MESH_ID)
         c.start()
         return c
-    ups, downs = n_z // 2, n_z - 1 - n_z // 2
     held = [send(z, core, partner, pr_send.at[0], pr_recv.at[0])]
     flying_up = send(z, core, up, up_send.at[0], up_recv.at[0])
     flying_dn = send(z, core, down, dn_send.at[0], dn_recv.at[0])
@@ -209,74 +222,93 @@
             if s < downs:
                 flying_dn = send(block, core, down, dn_send.at[s], dn_recv.at[s])
             held.append(send(block, core, partner, pr_send.at[ups + s], pr_recv.at[ups + s]))
+        if s > 1:
+            service(s - 2)
     for c in w_copies:
         c.wait()
     wj = jnp.concatenate([wbuf[c] for c in range(n_col)], axis=1)
-    wsel_out[...] = jnp.dot(wj, place[...], preferred_element_type=F32).astype(BF16)
+    chosen = jnp.dot(wj, place[...], preferred_element_type=F32)
+    m[n:n + rows, :] = chosen
     for c in held:
         c.wait()
     for b in range(n_z):
         for c in range(2):
             r0 = (b * 2 + c) * part
-            s_out[r0:r0 + part, :] = sblk[b, c]
-
-
-def exchange(idx, weight, inverse_rows, n_row, n_col):
+            m[r0:r0 + part, :] = sblk[b, c]
+    total = 2 * ups
+    done = [ups - 1]
+
+    def after(k):
+        goal = ups - 1 + ((k + 1) * (total - ups + 1)) // (n // BLOCK)
+        while done[0] < goal:
+            service(done[0])
+            done[0] += 1
+
+    eliminate(m, n, after)
+    solved = m[n:n + rows, :]
+    hi = solved.astype(BF16)
+    lo = (solved - hi.astype(F32)).astype(BF16)
+    prod = solved * jnp.dot(wj, place[...], preferred_element_type=F32)
+    folded = prod[:, 0:128]
+    for t in range(1, n // 128):
+        folded = folded + prod[:, t * 128:(t + 1) * 128]
+    sal_ref[...] = jnp.sum(folded.T, axis=0, keepdims=True) / (2.0 * n)
+    for c in mates:
+        c.wait()
+    both = jnp.concatenate([hi, lo], axis=0)
+    units = width // 256
+    cuts = [256 * (units * t // 4) for t in range(5)]
+    stores = []
+    for t in range(4):
+        cs, tile = slice(cuts[t], cuts[t + 1]), cuts[t + 1] - cuts[t]
+        gh = gat[0, :, :, :, cs].reshape(n, tile)
+        gl = gat[1, :, :, :, cs].reshape(n, tile)
+        a = jnp.dot(both, gh, preferred_element_type=F32)
+        acc = a[0:rows] + a[rows:2 * rows] + jnp.dot(hi, gl, preferred_element_type=F32)
+        outv[:, cs] = (w_ref[:, cs].astype(F32) - acc).astype(BF16)
+        c = pltpu.make_async_copy(outv.at[:, cs], out_ref.at[:, cs], out_sem.at[t])
+        c.start()
+        stores.append(c)
+    for c in stores:
+        c.wait()
+
+
+def step(idx, weight, inverse_rows, n_row, n_col):
     n = idx.shape[1]
-    rows, part = weight.shape[0], inverse_rows.shape[0]
+    rows, width = weight.shape
+    part = inverse_rows.shape[0]
     n_z = n_row // 2
     dma = pltpu.SemaphoreType.DMA
     vm = pl.BlockSpec(memory_space=pltpu.VMEM)
     return pl.pallas_call(
-        exchange_kernel,
-        out_shape=(jax.ShapeDtypeStruct((n, n), F32), jax.ShapeDtypeStruct((rows, n), BF16)),
+        step_kernel,
+        out_shape=(jax.ShapeDtypeStruct((rows, width), BF16), jax.ShapeDtypeStruct((1, rows), F32)),
         in_specs=[vm] * 3,
-        out_specs=(vm, vm),
+        out_specs=(pl.BlockSpec(memory_space=pl.ANY), vm),
         scratch_shapes=[
             pltpu.VMEM((n_col, part, LANES), F32),
             pltpu.VMEM((n_col, rows, LANES), BF16),
             pltpu.VMEM((n_col * LANES, n), BF16),
             pltpu.VMEM((n_z, 2, part, n), F32),
+            pltpu.VMEM((n + rows, n), F32),
+            pltpu.VMEM((2, n_z, 2, part, width), BF16),
+            pltpu.VMEM((rows, width), BF16),
             dma((n_col,)), dma((n_col,)), dma((n_col,)), dma((n_col,)),
             dma((n_z,)), dma((n_z,)), dma((n_z,)), dma((n_z,)), dma((n_z,)), dma((n_z,)),
+            dma((2, n_z)), dma((2, n_z)), dma((2, n_z)), dma((2, n_z)), dma((2, n_z)), dma((2, n_z)),
+            dma((4,)),
         ],
-        compiler_params=pltpu.CompilerParams(collective_id=0, has_side_effects=True),
-        name="exchange",
+        compiler_params=pltpu.CompilerParams(collective_id=0, has_side_effects=True, vmem_limit_bytes=60 << 20),
+        name="step",
     )(idx, weight, inverse_rows)
-
-
-def update_kernel(w_ref, inv_ref, hi_ref, lo_ref, out_ref):
-    inv = inv_ref[...]
-    ih = inv.astype(BF16)
-    il = (inv - ih.astype(F32)).astype(BF16)
-    hi, lo = hi_ref[...], lo_ref[...]
-    left = jnp.concatenate([hi, lo, hi], axis=1)
-    right = jnp.concatenate([ih, ih, il], axis=0)
-    out_ref[...] = (w_ref[...].astype(F32) - jnp.dot(left, right, preferred_element_type=F32)).astype(BF16)
-
-
-def update(weight, inverse_all, hi, lo, tile=256):
-    rows, width = weight.shape
-    n = hi.shape[1]
-    return pl.pallas_call(
-        update_kernel,
-        grid=(width // tile,),
-        out_shape=jax.ShapeDtypeStruct((rows, width), BF16),
-        in_specs=[pl.BlockSpec((rows, tile), lambda i: (0, i)), pl.BlockSpec((n, tile), lambda i: (0, i)),
-                  pl.BlockSpec((rows, n), lambda i: (0, 0)), pl.BlockSpec((rows, n), lambda i: (0, 0))],
-        out_specs=pl.BlockSpec((rows, tile), lambda i: (0, i)),
-        name="update",
-    )(weight, inverse_all, hi, lo)
 
 
 def solution(mesh):
     n_row, n_col = mesh.shape["row"], mesh.shape["col"]
 
     def body(weight, inverse_rows, pruned_index):
-        inverse_all = lax.all_gather(inverse_rows, "row", axis=0, tiled=True)
-        schur, chosen = exchange(pruned_index[None, :], weight, inverse_rows, n_row, n_col)
-        hi, lo, sal = solve(schur, chosen)
-        return update(weight, inverse_all, hi, lo), sal[:, 0]
+        out, sal = step(pruned_index[None, :], weight, inverse_rows, n_row, n_col)
+        return out, sal[0]
 
     return jax.shard_map(
         body,

time: 113 us -> 97.6 us (0.86)
  between operations: 14 us -> 0.65 us
  local copies, waits for them, and re-layouts: 0 us -> 3.32 us
  waiting for transfers between devices: 1.93 us -> 0 us
  Pallas kernels: 95.2 us -> 93.5 us
  other arithmetic: 1.58 us -> 0 us
    unnamed x0 -> x4, local copies, waits for them, and re-layouts: none -> 3.32 us
    pallas_call x3 -> x1, Pallas kernels: 95.2 us -> 93.5 us  [step(): pl.pallas_call(step_kernel, out_shape=(jax.ShapeDtypeStruct((rows, width)...]
    pallas_call x1 -> x0, other arithmetic: 1.58 us -> none  [solve(): pl.pallas_call(functools.partial(solve_kernel, B=B, n=n), out_shape=(jax....]
    all_gather x1 -> x0, waiting for transfers between devices: 1.25 us -> none  [body(): inverse_all = lax.all_gather(inverse_rows, 'row', axis=0, tiled=True)]
  transfers between devices with their start and end apart: 1 -> 0, of which waited for: 1 -> 0; matrix products, arithmetic and copies ran while one was open for 1% -> 0% of each run, Pallas kernels for 74% -> 0%
where the time goes in v2:
time: 97.6 us; the launch traced here: 97.4 us
  Pallas kernels  93.5 us (96%)
  local copies, waits for them, and re-layouts  3.32 us (3%)
    pallas_call x1, Pallas kernels, step(): pl.pallas_call(step_kernel, out_shape=(jax.ShapeDtypeStruct((rows, width)...  93.5 us
    unnamed x4, local copies, waits for them, and re-layouts  3.32 us

profile of v2, /device:TPU:1, one launch (start us, length us, event | category | flops | bytes accessed | tf_op | source)
XLA Modules:
  0.0 97.4 jit_solution(16536266337337705189)
XLA Ops:
  0.6 93.5 %step.1 = (bf16[256,3328]{1,0:T(8,128)(2,1)}, f32[1,256]{1,0:T(1,128)}) custom-call(s32[1,512]{1,0:T(1,128)} %bitcast.2, bf16[256,3328]{1,0:T(8,128)(2,1)} %w_ref.1, f32[16,3328]{1,0:T(8,128)} %inv_ref.1), custom_call_target="tpu_custom_call" | custom-call | tf_op jit(solution)/shard_map/step/pallas_call | solution.py:283
  94.1 0.0 copy-start
  94.1 2.7 %copy.7 = bf16[256,3328]{1,0:T(8,128)(2,1)} copy(bf16[256,3328]{1,0:T(8,128)(2,1)} %get-tuple-element.8) | data formatting | bytes 3407872
  96.9 0.0 copy-done
  96.9 0.6 copy.8
Async XLA Ops:
  94.1 2.8 %copy-start = (f32[1,256]{1,0:T(1,128)S(1)}, f32[1,256]{1,0:T(1,128)}, u32[]{:S(2)}) copy-start(f32[1,256]{1,0:T(1,128)} %get-tuple-element.5) | copy-start | bytes 3076

commit v3 on v2

--- a/solution.py
+++ b/solution.py
@@ -10,6 +10,8 @@
 F32, BF16 = jnp.float32, jnp.bfloat16
 LANES = 128
 BLOCK = 32
+PACE = (0, 1, 1, 1, 1, 1, 1, 1, 1)
+MID = (0, 1, 0, 1, 0, 1, 0, 1, 1)
 
 
 def split3(x):
@@ -67,37 +69,34 @@
     return P
 
 
-def eliminate(m, n, after):
-    rows = m.shape[0]
-    nb, nt = BLOCK // 8, n // 128
-    lane = lax.broadcasted_iota(jnp.int32, (8, 128), 1)
-    sub = lax.broadcasted_iota(jnp.int32, (8, 128), 0)
-    P = [[m[g*8:g*8+8, t*128:t*128+128] for t in range(nt)] for g in range(nb)]
-    for k in range(n // BLOCK):
-        kb = k * BLOCK
-        P = panel_gj(P, kb, nb, nt)
-        pt, l0 = kb // 128, kb % 128
-        for g in range(nb):
-            x = P[g][pt]
-            inside = (lane >= l0) & (lane < l0 + BLOCK)
-            eye = jnp.where(lane - l0 == sub + g * 8, 1.0, 0.0)
-            P[g][pt] = jnp.where(inside, eye - x, x)
-        U = jnp.concatenate([jnp.concatenate(P[g], axis=1) for g in range(nb)], axis=0)
-        uh, um, ul = split3(U)
-        us = jnp.concatenate([uh, um, uh, ul, um, uh], axis=0)
-
-        def upd(r0, r1):
-            C = m[r0:r1, pt*128:pt*128+128][:, l0:l0 + BLOCK]
-            ch, cm, cl = split3(C)
-            cs = jnp.concatenate([ch, ch, cm, ch, cm, cl], axis=1)
-            return m[r0:r1, :] - jnp.dot(cs, us, preferred_element_type=F32)
-        nr0 = (k + 1) * BLOCK
-        if k + 1 < n // BLOCK:
-            new = upd(nr0, nr0 + BLOCK)
-            P = [[new[g*8:g*8+8, t*128:t*128+128] for t in range(nt)] for g in range(nb)]
-            nr0 += BLOCK
-        m[nr0:rows, :] = upd(nr0, rows)
-        after(k)
+def stack_left(x):
+    h, m, l = split3(x)
+    return jnp.concatenate([h, h, m, h, m, l], axis=1)
+
+
+def pivot(rows, kb):
+    n = rows.shape[1]
+    nb, nt = BLOCK // 8, n // LANES
+    lane = lax.broadcasted_iota(jnp.int32, (8, LANES), 1)
+    sub = lax.broadcasted_iota(jnp.int32, (8, LANES), 0)
+    P = [[rows[g * 8:g * 8 + 8, t * LANES:(t + 1) * LANES] for t in range(nt)] for g in range(nb)]
+    P = panel_gj(P, kb, nb, nt)
+    pt, l0 = kb // LANES, kb % LANES
+    inside = (lane >= l0) & (lane < l0 + BLOCK)
+    upd, new = [], []
+    for g in range(nb):
+        eye = jnp.where(lane - l0 == sub + g * 8, 1.0, 0.0)
+        urow = [jnp.where(inside, eye - x, x) if t == pt else x for t, x in enumerate(P[g])]
+        nrow = [jnp.where(inside, x, -x) if t == pt else -x for t, x in enumerate(P[g])]
+        upd.append(jnp.concatenate(urow, axis=1))
+        new.append(jnp.concatenate(nrow, axis=1))
+    uh, um, ul = split3(jnp.concatenate(upd, axis=0))
+    return jnp.concatenate([uh, um, uh, ul, um, uh], axis=0), jnp.concatenate(new, axis=0)
+
+
+def reduced(x, kb, right):
+    return x - jnp.dot(stack_left(x[:, kb:kb + BLOCK]), right, preferred_element_type=F32)
+
 
 MESH_ID = pl.DeviceIdType.MESH
 
@@ -139,8 +138,8 @@
 
     ih, im, il = split3(inv_ref[...])
     part = inv_ref.shape[0]
-    gat[0, z, core] = ih
-    gat[1, z, core] = im
+    gat[0, 0, core] = ih
+    gat[1, 0, core] = im
     three = jnp.dot(jnp.concatenate([ih, im, il], axis=0), picker, preferred_element_type=F32)
     sbuf[col] = three[0:part] + three[part:2 * part] + three[2 * part:3 * part]
     wbuf[col] = jnp.dot(w_ref[...], picker, preferred_element_type=F32).astype(BF16)
@@ -149,8 +148,8 @@
     ups, downs = n_z // 2, n_z - 1 - n_z // 2
     sent = []
 
-    def push(p, block, target_row, send_sem, recv_sem):
-        c = pltpu.make_async_remote_copy(gat.at[p, block, core], gat.at[p, block, core], send_sem, recv_sem,
+    def push(p, block, landing, target_row, send_sem, recv_sem):
+        c = pltpu.make_async_remote_copy(gat.at[p, block % n_z, core], gat.at[p, landing % n_z, core], send_sem, recv_sem,
                                          device_id={"row": target_row, "col": col}, device_id_type=MESH_ID)
         c.start()
         return c
@@ -160,7 +159,8 @@
         c = pltpu.make_async_remote_copy(sbuf.at[col], sbuf.at[col], xs_send.at[k], xs_recv.at[k], device_id=target, device_id_type=MESH_ID)
         c.start()
         s_copies.append(c)
-    for k in range(1, n_col):
+
+    def give_w(k):
         target = {"row": row, "col": lax.rem(col + k, n_col)}
         c = pltpu.make_async_remote_copy(wbuf.at[col], wbuf.at[col], xw_send.at[k], xw_recv.at[k], device_id=target, device_id_type=MESH_ID)
         c.start()
@@ -168,29 +168,30 @@
 
     fly_up, fly_dn, mates = {}, {}, []
     for p in range(2):
-        fly_up[p] = push(p, z, up, gu_send.at[p, 0], gu_recv.at[p, 0])
-        fly_dn[p] = push(p, z, down, gd_send.at[p, 0], gd_recv.at[p, 0])
-        mates.append(push(p, z, partner, gp_send.at[p, 0], gp_recv.at[p, 0]))
+        fly_up[p] = push(p, 0, -1, up, gu_send.at[p, 0], gu_recv.at[p, 0])
+        fly_dn[p] = push(p, 0, 1, down, gd_send.at[p, 0], gd_recv.at[p, 0])
+        mates.append(push(p, 0, 0, partner, gp_send.at[p, 0], gp_recv.at[p, 0]))
 
     def service(piece):
         s, p = piece // 2 + 1, piece % 2
-        block = lax.rem(z + n_z - s, n_z)
         fly_up[p].wait()
         if s < ups:
-            fly_up[p] = push(p, block, up, gu_send.at[p, s], gu_recv.at[p, s])
-        mates.append(push(p, block, partner, gp_send.at[p, s], gp_recv.at[p, s]))
-        if s <= downs:
-            block = lax.rem(z + s, n_z)
+            fly_up[p] = push(p, -s, -s - 1, up, gu_send.at[p, s], gu_recv.at[p, s])
+        if s <= downs:
             fly_dn[p].wait()
             if s < downs:
-                fly_dn[p] = push(p, block, down, gd_send.at[p, s], gd_recv.at[p, s])
-            mates.append(push(p, block, partner, gp_send.at[p, ups + s], gp_recv.at[p, ups + s]))
+                fly_dn[p] = push(p, s, s + 1, down, gd_send.at[p, s], gd_recv.at[p, s])
+        mates.append(push(p, -s, -s, partner, gp_send.at[p, s], gp_recv.at[p, s]))
+        if s <= downs:
+            mates.append(push(p, s, s, partner, gp_send.at[p, ups + s], gp_recv.at[p, ups + s]))
 
     shard = lax.broadcasted_iota(jnp.int32, (n_col, n), 0)
     starts = jnp.sum(jnp.where(idx < shard * width, 1.0, 0.0), axis=1, keepdims=True)
     mine = (idx >= shard * width) & (idx < (shard + 1) * width)
     base = jnp.sum(jnp.where(mine, (shard * LANES).astype(F32) - starts, 0.0), axis=0, keepdims=True)
     slot_of = base + lax.broadcasted_iota(jnp.int32, (1, n), 1).astype(F32)
+    slot_of = pltpu.roll(jnp.broadcast_to(slot_of, (8, n)), lax.rem(n - BLOCK * z, n), 1)[0:1]
+    m[...] = jnp.zeros_like(m)
     for c in range(n_col):
         q = lax.broadcasted_iota(jnp.int32, (LANES, n), 0).astype(F32) + float(c * LANES)
         place[c * LANES:(c + 1) * LANES, :] = jnp.where(q == slot_of, 1.0, 0.0).astype(BF16)
@@ -200,59 +201,103 @@
     joined = jnp.concatenate([sbuf[c] for c in range(n_col)], axis=1)
     jh, jm, jl = split3(joined)
     three = jnp.dot(jnp.concatenate([jh, jm, jl], axis=0), place[...], preferred_element_type=F32)
-    sblk[z, core] = three[0:part] + three[part:2 * part] + three[2 * part:3 * part]
-
-    def send(block, owner_core, target_row, send_sem, recv_sem):
-        c = pltpu.make_async_remote_copy(sblk.at[block, owner_core], sblk.at[block, owner_core], send_sem, recv_sem,
+    sblk[0, core] = three[0:part] + three[part:2 * part] + three[2 * part:3 * part]
+
+    def send(block, landing, target_row, send_sem, recv_sem):
+        c = pltpu.make_async_remote_copy(sblk.at[block % n_z, core], sblk.at[landing % n_z, core], send_sem, recv_sem,
                                          device_id={"row": target_row, "col": col}, device_id_type=MESH_ID)
         c.start()
         return c
-    held = [send(z, core, partner, pr_send.at[0], pr_recv.at[0])]
-    flying_up = send(z, core, up, up_send.at[0], up_recv.at[0])
-    flying_dn = send(z, core, down, dn_send.at[0], dn_recv.at[0])
+
+    def turned(block):
+        both = jnp.concatenate([sblk[block % n_z, 0], sblk[block % n_z, 1]], axis=0)
+        shift = BLOCK * (block % n_z)
+        return pltpu.roll(both, shift, 1) if shift else both
+
+    done = [0]
+
+    def serve(count):
+        for _ in range(count):
+            if done[0] < 2 * ups:
+                service(done[0])
+                done[0] += 1
+
+    fly_s_up = send(0, -1, up, up_send.at[0], up_recv.at[0])
+    fly_s_dn = send(0, 1, down, dn_send.at[0], dn_recv.at[0])
+    fresh = {0: [send(0, 0, partner, pr_send.at[0], pr_recv.at[0])]}
+    column_at = lax.broadcasted_iota(jnp.int32, (2 * BLOCK, n), 1)
+
+    def take(s):
+        for c in fresh[s]:
+            c.wait()
+        if s == 0:
+            m[0:BLOCK, :] = pivot(turned(0), 0)[1]
+            serve(MID[s])
+            return
+        blocks = [n_z - s, s] if s <= downs else [n_z - s]
+        arrived = jnp.concatenate([turned(b) for b in blocks], axis=0)
+        count = arrived.shape[0]
+        known = (column_at[0:count] < BLOCK * s) | (column_at[0:count] >= n - BLOCK * (s - 1))
+        h, mid, low3 = split3(jnp.where(known, arrived, 0.0))
+        stack = jnp.concatenate([h, mid, low3], axis=0)
+        near = 4 * s <= n_z
+        spans = [(0, n // 4), (3 * n // 4, n)] if near else [(0, n)]
+        stack = jnp.concatenate([stack[:, a:b] for a, b in spans], axis=1)
+        mh, mm, ml = split3(jnp.concatenate([m[a:b, :] for a, b in spans], axis=0))
+        p1 = jnp.dot(stack, mh, preferred_element_type=F32)
+        p2 = jnp.dot(stack[0:2 * count], mm, preferred_element_type=F32)
+        p3 = jnp.dot(stack[0:count], ml, preferred_element_type=F32)
+        caught = p1[0:count] + ((p1[count:2 * count] + p2[0:count]) + ((p1[2 * count:] + p2[count:]) + p3))
+        arrived = jnp.where(known, 0.0, arrived) + caught
+        first = arrived[0:BLOCK]
+        low_end, high_end = BLOCK * s, n - BLOCK * (s - 1)
+        kb = BLOCK * (n_z - s)
+        right, new = pivot(first, kb)
+        if s <= downs:
+            second = reduced(arrived[BLOCK:], kb, right)
+        m[0:low_end, :] = reduced(m[0:low_end, :], kb, right)
+        if high_end < n:
+            m[high_end:n, :] = reduced(m[high_end:n, :], kb, right)
+        m[kb:kb + BLOCK, :] = new
+        serve(MID[s])
+        if s <= downs:
+            right, new = pivot(second, BLOCK * s)
+            m[0:low_end, :] = reduced(m[0:low_end, :], BLOCK * s, right)
+            m[kb:n, :] = reduced(m[kb:n, :], BLOCK * s, right)
+            m[BLOCK * s:BLOCK * s + BLOCK, :] = new
+
     for s in range(1, ups + 1):
-        block = lax.rem(z + n_z - s, n_z)
-        flying_up.wait()
+        fly_s_up.wait()
         if s < ups:
-            flying_up = send(block, core, up, up_send.at[s], up_recv.at[s])
-        held.append(send(block, core, partner, pr_send.at[s], pr_recv.at[s]))
-        if s <= downs:
-            block = lax.rem(z + s, n_z)
-            flying_dn.wait()
+            fly_s_up = send(-s, -s - 1, up, up_send.at[s], up_recv.at[s])
+        if s <= downs:
+            fly_s_dn.wait()
             if s < downs:
-                flying_dn = send(block, core, down, dn_send.at[s], dn_recv.at[s])
-            held.append(send(block, core, partner, pr_send.at[ups + s], pr_recv.at[ups + s]))
-        if s > 1:
-            service(s - 2)
+                fly_s_dn = send(s, s + 1, down, dn_send.at[s], dn_recv.at[s])
+        fresh[s] = [send(-s, -s, partner, pr_send.at[s], pr_recv.at[s])]
+        if s <= downs:
+            fresh[s].append(send(s, s, partner, pr_send.at[ups + s], pr_recv.at[ups + s]))
+        serve(PACE[s])
+        for k in range((s - 1) * (n_col - 1) // ups, s * (n_col - 1) // ups):
+            give_w(k + 1)
+        take(s - 1)
+    take(ups)
     for c in w_copies:
         c.wait()
     wj = jnp.concatenate([wbuf[c] for c in range(n_col)], axis=1)
     chosen = jnp.dot(wj, place[...], preferred_element_type=F32)
-    m[n:n + rows, :] = chosen
-    for c in held:
-        c.wait()
-    for b in range(n_z):
-        for c in range(2):
-            r0 = (b * 2 + c) * part
-            m[r0:r0 + part, :] = sblk[b, c]
-    total = 2 * ups
-    done = [ups - 1]
-
-    def after(k):
-        goal = ups - 1 + ((k + 1) * (total - ups + 1)) // (n // BLOCK)
-        while done[0] < goal:
-            service(done[0])
-            done[0] += 1
-
-    eliminate(m, n, after)
-    solved = m[n:n + rows, :]
+    picked_w = chosen.astype(BF16)
+    mh, mm, ml = split3(m[...])
+    solved = jnp.dot(picked_w, mh, preferred_element_type=F32) + (
+        jnp.dot(picked_w, mm, preferred_element_type=F32) + jnp.dot(picked_w, ml, preferred_element_type=F32))
     hi = solved.astype(BF16)
     lo = (solved - hi.astype(F32)).astype(BF16)
-    prod = solved * jnp.dot(wj, place[...], preferred_element_type=F32)
-    folded = prod[:, 0:128]
-    for t in range(1, n // 128):
-        folded = folded + prod[:, t * 128:(t + 1) * 128]
+    prod = solved * chosen
+    folded = prod[:, 0:LANES]
+    for t in range(1, n // LANES):
+        folded = folded + prod[:, t * LANES:(t + 1) * LANES]
     sal_ref[...] = jnp.sum(folded.T, axis=0, keepdims=True) / (2.0 * n)
+    serve(2 * ups)
     for c in mates:
         c.wait()
     both = jnp.concatenate([hi, lo], axis=0)
@@ -290,7 +335,7 @@
             pltpu.VMEM((n_col, rows, LANES), BF16),
             pltpu.VMEM((n_col * LANES, n), BF16),
             pltpu.VMEM((n_z, 2, part, n), F32),
-            pltpu.VMEM((n + rows, n), F32),
+            pltpu.VMEM((n, n), F32),
             pltpu.VMEM((2, n_z, 2, part, width), BF16),
             pltpu.VMEM((rows, width), BF16),
             dma((n_col,)), dma((n_col,)), dma((n_col,)), dma((n_col,)),

time: 97.6 us -> 77.6 us (0.80)
  Pallas kernels: 93.5 us -> 73.4 us
    pallas_call x1, Pallas kernels: 93.5 us -> 73.4 us  [step(): pl.pallas_call(step_kernel, out_shape=(jax.ShapeDtypeStruct((rows, width)...]
where the time goes in v3:
time: 77.6 us; the launch traced here: 77.4 us
  Pallas kernels  73.4 us (95%)
  local copies, waits for them, and re-layouts  3.32 us (4%)
    pallas_call x1, Pallas kernels, step(): pl.pallas_call(step_kernel, out_shape=(jax.ShapeDtypeStruct((rows, width)...  73.4 us
    unnamed x4, local copies, waits for them, and re-layouts  3.32 us

profile of v3, /device:TPU:1, one launch (start us, length us, event | category | flops | bytes accessed | tf_op | source)
XLA Modules:
  0.0 77.4 jit_solution(17898160967139962174)
XLA Ops:
  0.6 73.4 %step.1 = (bf16[256,3328]{1,0:T(8,128)(2,1)}, f32[1,256]{1,0:T(1,128)}) custom-call(s32[1,512]{1,0:T(1,128)} %bitcast.2, bf16[256,3328]{1,0:T(8,128)(2,1)} %w_ref.1, f32[16,3328]{1,0:T(8,128)} %inv_ref.1), custom_call_target="tpu_custom_call" | custom-call | tf_op jit(solution)/shard_map/step/pallas_call | solution.py:328
  74.1 0.0 copy-start
  74.1 2.7 %copy.7 = bf16[256,3328]{1,0:T(8,128)(2,1)} copy(bf16[256,3328]{1,0:T(8,128)(2,1)} %get-tuple-element.8) | data formatting | bytes 3407872
  76.8 0.0 copy-done
  76.8 0.6 copy.8
Async XLA Ops:
  74.1 2.8 %copy-start = (f32[1,256]{1,0:T(1,128)S(1)}, f32[1,256]{1,0:T(1,128)}, u32[]{:S(2)}) copy-start(f32[1,256]{1,0:T(1,128)} %get-tuple-element.5) | copy-start | bytes 3076

commit v4 on v3

--- a/solution.py
+++ b/solution.py
@@ -10,7 +10,7 @@
 F32, BF16 = jnp.float32, jnp.bfloat16
 LANES = 128
 BLOCK = 32
-PACE = (0, 1, 1, 1, 1, 1, 1, 1, 1)
+PACE = (2, 0, 1, 1, 1, 1, 1, 1, 1)
 MID = (0, 1, 0, 1, 0, 1, 0, 1, 1)
 
 
@@ -101,12 +101,12 @@
 MESH_ID = pl.DeviceIdType.MESH
 
 
-def step_kernel(idx_ref, w_ref, inv_ref, out_ref, sal_ref, sbuf, wbuf, place, sblk, m, gat, outv,
+def step_kernel(idx_ref, w_hbm, inv_ref, out_ref, sal_ref, sbuf, wbuf, place, sblk, m, gat, outv, w_ref, load_sem,
                 xs_send, xs_recv, xw_send, xw_recv, up_send, up_recv, dn_send, dn_recv, pr_send, pr_recv,
                 gu_send, gu_recv, gd_send, gd_recv, gp_send, gp_recv, out_sem):
     n_row, n_col = lax.axis_size("row"), lax.axis_size("col")
     n_z = n_row // 2
-    rows, width = w_ref.shape
+    rows, width = w_hbm.shape
     n = idx_ref.shape[1]
     row, col = lax.axis_index("row"), lax.axis_index("col")
     z, core = row // 2, lax.rem(row, 2)
@@ -120,6 +120,8 @@
     for other in (up, down, partner):
         pl.semaphore_signal(barrier, inc=1, device_id={"row": other, "col": col}, device_id_type=MESH_ID)
 
+    load = pltpu.make_async_copy(w_hbm, w_ref, load_sem)
+    load.start()
     idx = idx_ref[...]
     anchor = col * width
     start = jnp.sum(jnp.where(idx < anchor, 1.0, 0.0), axis=1, keepdims=True)
@@ -142,6 +144,7 @@
     gat[1, 0, core] = im
     three = jnp.dot(jnp.concatenate([ih, im, il], axis=0), picker, preferred_element_type=F32)
     sbuf[col] = three[0:part] + three[part:2 * part] + three[2 * part:3 * part]
+    load.wait()
     wbuf[col] = jnp.dot(w_ref[...], picker, preferred_element_type=F32).astype(BF16)
 
     pl.semaphore_wait(barrier, n_col + 2)
@@ -174,15 +177,16 @@
 
     def service(piece):
         s, p = piece // 2 + 1, piece % 2
-        fly_up[p].wait()
-        if s < ups:
-            fly_up[p] = push(p, -s, -s - 1, up, gu_send.at[p, s], gu_recv.at[p, s])
-        if s <= downs:
+        if s < ups or p == 0:
+            fly_up[p].wait()
+            if s + 1 < ups or (s + 1 == ups and p == 0):
+                fly_up[p] = push(p, -s, -s - 1, up, gu_send.at[p, s], gu_recv.at[p, s])
+        if s < ups or p == 1:
             fly_dn[p].wait()
-            if s < downs:
+            if s + 1 < ups or (s + 1 == ups and p == 1):
                 fly_dn[p] = push(p, s, s + 1, down, gd_send.at[p, s], gd_recv.at[p, s])
         mates.append(push(p, -s, -s, partner, gp_send.at[p, s], gp_recv.at[p, s]))
-        if s <= downs:
+        if s < ups:
             mates.append(push(p, s, s, partner, gp_send.at[p, ups + s], gp_recv.at[p, ups + s]))
 
     shard = lax.broadcasted_iota(jnp.int32, (n_col, n), 0)
@@ -225,6 +229,7 @@
     fly_s_up = send(0, -1, up, up_send.at[0], up_recv.at[0])
     fly_s_dn = send(0, 1, down, dn_send.at[0], dn_recv.at[0])
     fresh = {0: [send(0, 0, partner, pr_send.at[0], pr_recv.at[0])]}
+    serve(PACE[0])
     column_at = lax.broadcasted_iota(jnp.int32, (2 * BLOCK, n), 1)
 
     def take(s):
@@ -328,7 +333,7 @@
     return pl.pallas_call(
         step_kernel,
         out_shape=(jax.ShapeDtypeStruct((rows, width), BF16), jax.ShapeDtypeStruct((1, rows), F32)),
-        in_specs=[vm] * 3,
+        in_specs=[vm, pl.BlockSpec(memory_space=pl.ANY), vm],
         out_specs=(pl.BlockSpec(memory_space=pl.ANY), vm),
         scratch_shapes=[
             pltpu.VMEM((n_col, part, LANES), F32),
@@ -338,6 +343,8 @@
             pltpu.VMEM((n, n), F32),
             pltpu.VMEM((2, n_z, 2, part, width), BF16),
             pltpu.VMEM((rows, width), BF16),
+            pltpu.VMEM((rows, width), BF16),
+            dma,
             dma((n_col,)), dma((n_col,)), dma((n_col,)), dma((n_col,)),
             dma((n_z,)), dma((n_z,)), dma((n_z,)), dma((n_z,)), dma((n_z,)), dma((n_z,)),
             dma((2, n_z)), dma((2, n_z)), dma((2, n_z)), dma((2, n_z)), dma((2, n_z)), dma((2, n_z)),
@@ -348,11 +355,39 @@
     )(idx, weight, inverse_rows)
 
 
+def settle_kernel(o_ref, s_ref, out_ref, sal_ref, buf, in_sem, out_sem):
+    parts = buf.shape[0]
+    rows = buf.shape[1]
+    ins = [pltpu.make_async_copy(o_ref.at[i * rows:(i + 1) * rows, :], buf.at[i], in_sem.at[i]) for i in range(parts)]
+    outs = [pltpu.make_async_copy(buf.at[i], out_ref.at[i * rows:(i + 1) * rows, :], out_sem.at[i]) for i in range(parts)]
+    for c in ins:
+        c.start()
+    sal_ref[...] = s_ref[...]
+    for i in range(parts):
+        ins[i].wait()
+        outs[i].start()
+    for c in outs:
+        c.wait()
+
+
+def settle(out, sal, parts=8):
+    anyspace, vm = pl.BlockSpec(memory_space=pl.ANY), pl.BlockSpec(memory_space=pltpu.VMEM)
+    return pl.pallas_call(
+        settle_kernel,
+        out_shape=(jax.ShapeDtypeStruct(out.shape, out.dtype), jax.ShapeDtypeStruct(sal.shape, sal.dtype)),
+        in_specs=[anyspace, vm],
+        out_specs=(anyspace, vm),
+        scratch_shapes=[pltpu.VMEM((parts, out.shape[0] // parts, out.shape[1]), out.dtype),
+                        pltpu.SemaphoreType.DMA((parts,)), pltpu.SemaphoreType.DMA((parts,))],
+        name="settle",
+    )(out, sal)
+
+
 def solution(mesh):
     n_row, n_col = mesh.shape["row"], mesh.shape["col"]
 
     def body(weight, inverse_rows, pruned_index):
-        out, sal = step(pruned_index[None, :], weight, inverse_rows, n_row, n_col)
+        out, sal = settle(*step(pruned_index[None, :], weight, inverse_rows, n_row, n_col))
         return out, sal[0]
 
     return jax.shard_map(

time: 77.6 us -> 76.5 us (0.986)
  local copies, waits for them, and re-layouts: 3.32 us -> 0 us
  Pallas kernels: 73.4 us -> 75.5 us
    pallas_call x0 -> x1, Pallas kernels: none -> 3.59 us  [settle(): pl.pallas_call(settle_kernel, out_shape=(jax.ShapeDtypeStruct(out.shape,...]
    unnamed x4 -> x0, local copies, waits for them, and re-layouts: 3.32 us -> none
    pallas_call x1, Pallas kernels: 73.4 us -> 71.9 us  [step(): pl.pallas_call(step_kernel, out_shape=(jax.ShapeDtypeStruct((rows, width)...]
where the time goes in v4:
time: 76.5 us; the launch traced here: 76.3 us
  Pallas kernels  75.5 us (99%)
  between operations  0.8 us (1%)
    pallas_call x1, Pallas kernels, step(): pl.pallas_call(step_kernel, out_shape=(jax.ShapeDtypeStruct((rows, width)...  71.9 us
    pallas_call x1, Pallas kernels, settle(): pl.pallas_call(settle_kernel, out_shape=(jax.ShapeDtypeStruct(out.shape,...  3.59 us

profile of v4, /device:TPU:1, one launch (start us, length us, event | category | flops | bytes accessed | tf_op | source)
XLA Modules:
  0.0 76.3 jit_solution(18282236006969606304)
XLA Ops:
  0.6 71.9 %step.1 = (bf16[256,3328]{1,0:T(8,128)(2,1)}, f32[1,256]{1,0:T(1,128)}) custom-call(s32[1,512]{1,0:T(1,128)} %bitcast.2, bf16[256,3328]{1,0:T(8,128)(2,1)} %w_hbm.1, f32[16,3328]{1,0:T(8,128)} %inv_ref.1), custom_call_target="tpu_custom_call" | custom-call | tf_op jit(solution)/shard_map/step/pallas_call | solution.py:333
  72.6 3.6 %settle.1 = (bf16[256,3328]{1,0:T(8,128)(2,1)}, f32[1,256]{1,0:T(1,128)}) custom-call(bf16[256,3328]{1,0:T(8,128)(2,1)} %get-tuple-element.6.o_ref, f32[1,256]{1,0:T(1,128)} %get-tuple-element.7.s_ref), custom_call_target="tpu_custom_call" | custom-call | tf_op jit(solution)/shard_map/settle/pallas_call | solution.py:375

commit v5 on v4

--- a/solution.py
+++ b/solution.py
@@ -11,7 +11,7 @@
 LANES = 128
 BLOCK = 32
 PACE = (2, 0, 1, 1, 1, 1, 1, 1, 1)
-MID = (0, 1, 0, 1, 0, 1, 0, 1, 1)
+MID = (0, 1, 0, 1, 1, 1, 0, 1, 1)
 
 
 def split3(x):

time: 76.5 us -> 76.3 us (level)
  no operation moved by 1% of the time
where the time goes in v5:
time: 76.3 us; the launch traced here: 76 us
  Pallas kernels  75.2 us (99%)
  between operations  0.8 us (1%)
    pallas_call x1, Pallas kernels, step(): pl.pallas_call(step_kernel, out_shape=(jax.ShapeDtypeStruct((rows, width)...  71.6 us
    pallas_call x1, Pallas kernels, settle(): pl.pallas_call(settle_kernel, out_shape=(jax.ShapeDtypeStruct(out.shape,...  3.59 us

profile of v5, /device:TPU:1, one launch (start us, length us, event | category | flops | bytes accessed | tf_op | source)
XLA Modules:
  0.0 76.0 jit_solution(11116908526871350204)
XLA Ops:
  0.6 71.6 %step.1 = (bf16[256,3328]{1,0:T(8,128)(2,1)}, f32[1,256]{1,0:T(1,128)}) custom-call(s32[1,512]{1,0:T(1,128)} %bitcast.2, bf16[256,3328]{1,0:T(8,128)(2,1)} %w_hbm.1, f32[16,3328]{1,0:T(8,128)} %inv_ref.1), custom_call_target="tpu_custom_call" | custom-call | tf_op jit(solution)/shard_map/step/pallas_call | solution.py:333
  72.3 3.6 %settle.1 = (bf16[256,3328]{1,0:T(8,128)(2,1)}, f32[1,256]{1,0:T(1,128)}) custom-call(bf16[256,3328]{1,0:T(8,128)(2,1)} %get-tuple-element.6.o_ref, f32[1,256]{1,0:T(1,128)} %get-tuple-element.7.s_ref), custom_call_target="tpu_custom_call" | custom-call | tf_op jit(solution)/shard_map/settle/pallas_call | solution.py:375
